TPU v7x, 512 devices: a whole 4x8x8 slice. The times are simulated.
512 devices in a mesh: group: 16 (over y, core), inner: 32 (over x, z).
Axes of the slice: x: 4, y: 8, z: 8, core: 2. Of those that a mesh axis runs over, the one named last changes fastest.
Arguments:
- pair_rows: bfloat16 [8192, 2048], P(('group', 'inner')), may hold values from -6 to 6
- group_ids: int32 [8192, 1], P(('group', 'inner')), may hold values from 0 to 15; in each aligned block of 16 rows (0 to 15, 16 to 31, ...) at most 2 rows name the same one
- local_ids: int32 [8192, 1], P(('group', 'inner')), may hold values from 0 to 1
- route_weight: float32 [8192], P(('group', 'inner')), may hold values from 0.3 to 1
- w_up: bfloat16 [32, 2048, 8192], P('group', None, 'inner'), may hold values from -0.125 to 0.125
- w_down: bfloat16 [32, 8192, 2048], P('group', 'inner'), may hold values from -0.0625 to 0.0625
Outputs:
- mixed: bfloat16 [8192, 2048], P(('group', 'inner'))
Inputs may be any that keep to these rules, and one draw needn't show every extreme that they name: `group_ids`: among the rows of one device no value is named more than 2 times, a bound that some block reaches.
All inputs are finite; a program needn't handle non-finite values.
Results may differ from a plain program's by a relative error of at most 0.02.
Values may be sent and summed in bfloat16 or wider, within the bound.
A program may use at most 64 MiB of HBM per device.

v0:
```python
import jax
import jax.numpy as jnp
from jax import lax
from jax.sharding import PartitionSpec as P


def body(pair_rows, group_ids, local_ids, route_weight, w_up, w_down):
    groups = lax.axis_size("group")
    inner_size = lax.axis_size("inner")
    count_rows = pair_rows.shape[0]
    model_width = pair_rows.shape[1]
    local_count = w_up.shape[0]
    capacity = 2 * count_rows // groups
    group_of = group_ids[:, 0]
    onehot = (group_of[:, None] == jnp.arange(groups, dtype=jnp.int32)[None, :]).astype(jnp.int32)
    rank_in = jnp.sum((jnp.cumsum(onehot, 0) - onehot) * onehot, 1)
    target = group_of * capacity + rank_in
    placing = (jnp.arange(groups * capacity, dtype=jnp.int32)[:, None] == target[None, :]).astype(
        jnp.bfloat16
    )
    outgoing = jnp.dot(placing, pair_rows, preferred_element_type=jnp.float32).astype(jnp.bfloat16)
    outgoing = outgoing.reshape(1, groups, capacity, model_width)
    tag_rows = (local_ids[:, 0] + 1).astype(jnp.bfloat16)
    tags = jnp.dot(placing, tag_rows, preferred_element_type=jnp.float32).astype(jnp.bfloat16)
    tags = tags.reshape(1, groups, capacity)
    arrived, arrived_tags = (
        lax.all_to_all(outgoing, "group", split_axis=1, concat_axis=1, tiled=True),
        lax.all_to_all(tags, "group", split_axis=1, concat_axis=1, tiled=True),
    )
    gathered, gathered_tags = (
        lax.all_gather(arrived, "inner", axis=0, tiled=True),
        lax.all_gather(arrived_tags, "inner", axis=0, tiled=True),
    )
    slots = gathered.reshape(inner_size * groups * capacity, model_width)
    slot_tags = gathered_tags.reshape(inner_size * groups * capacity).astype(jnp.float32)
    expert_index = jnp.arange(local_count, dtype=jnp.float32) + 1.0
    own_rows = groups * capacity
    selector = (slot_tags[:, None] == expert_index[None, :]).astype(jnp.float32)
    up_val = jnp.einsum("rd,edf->ref", slots, w_up, preferred_element_type=jnp.float32)
    hidden = (jax.nn.silu(up_val) * selector[:, :, None]).astype(jnp.bfloat16)
    every_term = jnp.einsum("ref,efd->rd", hidden, w_down, preferred_element_type=jnp.float32)
    totals = lax.psum(every_term.astype(jnp.bfloat16), "inner").astype(jnp.float32)
    summed = lax.dynamic_slice_in_dim(totals, lax.axis_index("inner") * own_rows, own_rows, 0)
    send_back = summed.astype(jnp.bfloat16).reshape(groups, capacity, model_width)
    returned = lax.all_to_all(send_back, "group", split_axis=0, concat_axis=0, tiled=True)
    combined = jnp.dot(
        placing.T,
        returned.reshape(groups * capacity, model_width),
        preferred_element_type=jnp.float32,
    )
    return (combined * route_weight[:, None]).astype(jnp.bfloat16)


def solution(mesh):
    placed = (
        P(("group", "inner"), None),
        P(("group", "inner"), None),
        P(("group", "inner"), None),
        P(("group", "inner")),
        P("group", None, "inner"),
        P("group", "inner", None),
    )
    return jax.shard_map(
        body, mesh=mesh, in_specs=placed, out_specs=P(("group", "inner"), None), check_vma=False
    )
```

profile of v0, /device:TPU:1, one launch (start us, length us, event | category | flops | bytes accessed | tf_op | source)
XLA Modules:
  0.0 338.9 jit_solution(1572055282033931939)
XLA Ops:
  6.5 0.9 fusion.5
  7.5 0.8 select_reduce_fusion
  8.3 0.7 multiply_add_fusion
  9.0 1.0 convolution_convert_fusion
  10.0 0.1 reshape.67
  10.1 18.5 %all_to_all.15 = bf16[1,16,2,2048]{3,2,0,1:T(2,128)(2,1)S(1)} all-to-all(bf16[1,16,2,2048]{3,2,0,1:T(2,128)(2,1)S(1)} %bitcast.15), channel_id=1, replica_groups=mesh['group'=16,'inner'=32] {'group'}, dimensions={1} | all-to-all | bytes 262144 | tf_op jit(solution)/shard_map/all_to_all | solution.py:27
  28.6 0.7 copy.14
  29.3 0.8 fusion.1
  30.1 0.7 reshape.78
  30.8 3.4 all-to-all-start.1
  34.2 6.5 %all-to-all-done.1 = bf16[1,16,2]{2,0,1:T(2,128)(2,1)S(1)} async-done(((bf16[1,16,2]{2,0,1:T(2,128)(2,1)}), bf16[1,16,2]{2,0,1:T(2,128)(2,1)S(1)}, u32[]{:S(2)}, u32[]{:S(2)}) %all-to-all-start.1) | async-done | bytes 96 | tf_op jit(solution)/shard_map/all_to_all | solution.py:28
  40.7 0.1 copy.17
  40.8 37.2 %all_gather.7 = bf16[32,16,2]{1,2,0:T(2,128)(2,1)S(1)} all-gather(bf16[1,16,2]{1,2,0:T(2,128)(2,1)S(1)} %copy.17), channel_id=1, replica_groups=mesh['group'=16,'inner'=32] {'inner'}, dimensions={0}, use_global_device_ids=true | all-gather | bytes 2112 | tf_op jit(solution)/shard_map/all_gather | solution.py:32
  78.1 0.2 copy.19
  78.3 0.2 reshape.72
  78.5 34.5 %all-gather.2.cloned.1.call-done = bf16[32,16,2,2048]{3,1,2,0:T(8,128)(2,1)} async-done(((bf16[1,16,2,2048]{3,1,2,0:T(8,128)(2,1)}), bf16[32,16,2,2048]{3,1,2,0:T(8,128)(2,1)}) %all-gather.2.cloned.1.call-update) | async-done | bytes 4194320 | tf_op jit(solution)/shard_map/all_gather | solution.py:31
  113.1 8.5 %copy.15 = bf16[32,16,2,2048]{3,2,1,0:T(2,128)(2,1)} copy(bf16[32,16,2,2048]{3,1,2,0:T(8,128)(2,1)} %all-gather.2.cloned.1.call-done) | data formatting | bytes 8388608 | tf_op jit(solution)/shard_map/all_gather | solution.py:31
  121.6 7.2 %reshape.73 = bf16[1024,2048,1]{1,0,2:T(8,128)(2,1)} reshape(bf16[32,16,2,2048]{3,2,1,0:T(2,128)(2,1)} %copy.15) | data formatting | bytes 8388608 | tf_op jit(solution)/shard_map/reshape | solution.py:34
  128.8 9.5 %bitcast_convert_fusion = bf16[1024,2048]{1,0:T(8,128)(2,1)} fusion(bf16[2,256,2048]{2,1,0:T(8,128)(2,1)S(1)} %copy-done, bf16[1024,2048,1]{1,0,2:T(8,128)(2,1)} %reshape.73, bf16[2,2048,256]{2,1,0:T(8,128)(2,1)} %param.10, f32[1024,2]{0,1:T(2,128)S(1)} %compare_convert_fusion), kind=kOutput, calls=%fused_computation | convolution fusion | flops 4300210176 | bytes 12591104 | tf_op jit(solution)/shard_map/ref,efd->rd/dot_general | solution.py:41
  138.4 172.9 %all-reduce.2.cloned.1.call-done = bf16[1024,2048]{1,0:T(8,128)(2,1)} async-done(((bf16[1024,2048]{1,0:T(8,128)(2,1)}), bf16[1024,2048]{1,0:T(8,128)(2,1)}) %all-reduce.2.cloned.1.call-update) | async-done | bytes 4194320 | tf_op jit(solution)/shard_map/psum | solution.py:42
  311.2 0.9 convert_convert_fusion
  312.1 0.1 reshape.70
  312.2 19.0 %all_to_all.16 = bf16[16,2,2048]{2,1,0:T(2,128)(2,1)S(1)} all-to-all(bf16[16,2,2048]{2,1,0:T(2,128)(2,1)S(1)} %reshape.70), channel_id=1, replica_groups=mesh['group'=16,'inner'=32] {'group'}, dimensions={0} | all-to-all | bytes 262144 | tf_op jit(solution)/shard_map/all_to_all | solution.py:45
  331.3 0.8 fusion
  (13 shorter events, 0.3 us)
Async XLA Ops:
  6.5 122.3 %copy-start = (bf16[2,256,2048]{2,1,0:T(8,128)(2,1)S(1)}, bf16[2,256,2048]{2,1,0:T(8,128)(2,1)}, u32[]{:S(2)}) copy-start(bf16[2,256,2048]{2,1,0:T(8,128)(2,1)} %param.11) | copy-start | bytes 6291460
  6.5 106.6 %all-gather.2.cloned.1.call-start = ((), (), s32[]{:S(2)}) async-start(), calls=%async_computation.3 | async-start | bytes 4325376 | tf_op jit(solution)/shard_map/all_gather | solution.py:31
  30.8 9.9 %all-to-all-start.1 = ((bf16[1,16,2]{2,0,1:T(2,128)(2,1)}), bf16[1,16,2]{2,0,1:T(2,128)(2,1)S(1)}, u32[]{:S(2)}, u32[]{:S(2)}) async-start(bf16[1,16,2]{2,0,1:T(2,128)(2,1)} %reshape.78), calls=%async_computation.1 | async-start | bytes 16384 | tf_op jit(solution)/shard_map/all_to_all | solution.py:28
  34.1 277.1 %all-reduce.2.cloned.1.call-start = ((), (), s32[]{:S(2)}) async-start(), calls=%async_computation.4 | async-start | bytes 8388608 | tf_op jit(solution)/shard_map/psum | solution.py:42
  138.3 192.9 %copy-start.1 = (f32[16]{0:T(128)S(1)}, f32[16]{0:T(128)}, u32[]{:S(2)}) copy-start(f32[16]{0:T(128)} %param.9) | copy-start | bytes 196
Sparse Core Ops, SparseCore 0:
  29.4 83.6 all-gather.1
  138.5 172.6 all-reduce.1
where the time goes:
time: 339 us
  waiting for transfers between devices  214 us (63%)
  blocking collectives  74.7 us (22%)
  local copies, waits for them, and re-layouts  17.9 us (5%)
  between operations  13.5 us (4%)
  matrix products  12.1 us (4%)
  starting transfers between devices  3.41 us (1%)
  other arithmetic  3.41 us (1%)
    psum x1, waiting for transfers between devices, body(): lax.psum(every_term.astype(jnp.bfloat16), 'inner').astype(jnp.float32)  173 us
    all_gather x1, blocking collectives, body(): lax.all_gather(arrived_tags, 'inner', axis=0, tiled=True)  37.2 us
    all_gather x1, waiting for transfers between devices, body(): lax.all_gather(arrived, 'inner', axis=0, tiled=True)  34.5 us
    all_to_all x1, blocking collectives, body(): lax.all_to_all(send_back, 'group', split_axis=0, concat_axis=0, tiled=True)  19 us
    all_to_all x1, blocking collectives, body(): lax.all_to_all(outgoing, 'group', split_axis=1, concat_axis=1, tiled=True)  18.5 us
    dot_general x1, matrix products, body(): jnp.einsum('ref,efd->rd', hidden, w_down, preferred_element_type=jnp.floa...  9.51 us
    all_gather x1, local copies, waits for them, and re-layouts, body(): lax.all_gather(arrived, 'inner', axis=0, tiled=True)  8.52 us
    reshape x1, local copies, waits for them, and re-layouts, body(): slots = gathered.reshape(inner_size * groups * capacity, model_width)  7.19 us
  transfers between devices with their start and end apart: 3, of which 3 were waited for; matrix products, arithmetic and copies ran while one was open for 1% of the time, Pallas kernels for 0%

commit v1 on v0

v1 whole, which is shorter than its diff:
```python
import functools

import jax
import jax.numpy as jnp
from jax import lax
from jax.experimental import pallas as pl
from jax.experimental.pallas import tpu as pltpu
from jax.sharding import PartitionSpec as P

MESH = pl.DeviceIdType.MESH
XS, ZS = 4, 8
TAG = 128
f32, bf16 = jnp.float32, jnp.bfloat16


def kernel(
    rows_ref, gid_ref, lid_ref, rw_ref, wup_hbm, wdn_hbm, o_ref,
    wup, wdn, wsem,
    out_buf, in_buf, a2a_s, a2a_r,
    xa, xb, a1_s, a1_r, a2_s, a2_r, b1_s, b1_r, b2_s, b2_r,
    pa, pb, ra_s, ra_r, ra_buf, rax_s, rax_r, rax_out, rax_in,
    rbx_s, rbx_r, rbx_in, rb_s, rb_r, rb_buf, rb_out,
    ret_out, ret_in, ret_s, ret_r,
):
    n_rows, width = rows_ref.shape
    groups, cap = out_buf.shape[0], out_buf.shape[1]
    slots = groups * cap
    half = slots // 2
    g = lax.axis_index("group")
    i = lax.axis_index("inner")
    x, z = i // ZS, i % ZS

    def inner_at(xx, zz):
        return lax.rem(xx + XS, XS) * ZS + lax.rem(zz + ZS, ZS)

    right, left = inner_at(x, z + 1), inner_at(x, z - 1)

    def zat(d):
        return lax.rem(z + d + ZS, ZS)

    def xat(k):
        return lax.rem(x + k, XS)

    sent = []

    def send(src, dst, s, r, dev):
        c = pltpu.make_async_remote_copy(
            src_ref=src, dst_ref=dst, send_sem=s, recv_sem=r, device_id=dev, device_id_type=MESH
        )
        c.start()
        sent.append(c)

    def arrived(dst, s, r):
        pltpu.make_async_remote_copy(
            src_ref=dst, dst_ref=dst, send_sem=s, recv_sem=r, device_id=(g, right), device_id_type=MESH
        ).wait_recv()

    cw = [
        pltpu.make_async_copy(wup_hbm, wup, wsem.at[0]),
        pltpu.make_async_copy(wdn_hbm, wdn, wsem.at[1]),
    ]
    for c in cw:
        c.start()

    barrier = pltpu.get_barrier_semaphore()

    @pl.loop(1, groups)
    def _(k):
        pl.semaphore_signal(barrier, inc=1, device_id=(lax.rem(g + k, groups), i), device_id_type=MESH)

    for k in range(1, XS):
        pl.semaphore_signal(barrier, inc=1, device_id=(g, inner_at(x + k, z)), device_id_type=MESH)
    for dev in (right, left):
        pl.semaphore_signal(barrier, inc=1, device_id=(g, dev), device_id_type=MESH)

    gid = gid_ref[...]
    sub = lax.broadcasted_iota(jnp.int32, (n_rows, n_rows), 0)
    lane = lax.broadcasted_iota(jnp.int32, (n_rows, n_rows), 1)
    eye = sub == lane
    gcol = jnp.sum(jnp.where(eye, gid, 0), axis=1, keepdims=True)
    before_row = jnp.where((gcol == gid) & (sub < lane), 1, 0)
    target = gid * cap + jnp.sum(before_row, axis=0, keepdims=True)
    target_col = jnp.sum(jnp.where(eye, target, 0), axis=1, keepdims=True)
    places = lax.broadcasted_iota(jnp.int32, (slots, n_rows), 0) == target
    out_rows = jnp.dot(
        jnp.where(places, 1.0, 0.0).astype(bf16), rows_ref[...], preferred_element_type=f32
    ).astype(bf16)
    tags = jnp.sum(jnp.where(places, lid_ref[...], 0), axis=1, keepdims=True).astype(f32)
    out_tags = jnp.broadcast_to(tags, (slots, TAG)).astype(bf16)
    for d in range(groups):
        out_buf[d, :, :width] = out_rows[cap * d : cap * (d + 1)]
        out_buf[d, :, width:] = out_tags[cap * d : cap * (d + 1)]

    pl.semaphore_wait(barrier, groups - 1 + XS - 1 + 2)

    @pl.loop(1, groups)
    def _(k):
        d = lax.rem(g + k, groups)
        pltpu.make_async_remote_copy(
            src_ref=out_buf.at[d], dst_ref=in_buf.at[g], send_sem=a2a_s.at[d], recv_sem=a2a_r.at[g],
            device_id=(d, i), device_id_type=MESH,
        ).start()

    in_buf[g] = out_buf[g]

    @pl.loop(1, groups)
    def _(k):
        d = lax.rem(g + k, groups)
        arrived(in_buf.at[d], a2a_s.at[d], a2a_r.at[d])

    for d in range(groups // 2):
        xa[z, x, cap * d : cap * (d + 1), :] = in_buf[d]
        xb[x, z, cap * d : cap * (d + 1), :] = in_buf[d + groups // 2]

    def spread_b(zz):
        for k in range(1, XS):
            send(xb.at[x, zz], xb.at[x, zz], b2_s.at[k, zz], b2_r.at[x, zz], (g, inner_at(x + k, z)))

    send(xb.at[x, z], xb.at[x, z], b1_s.at[0, 0], b1_r.at[0, 0], (g, right))
    send(xb.at[x, z], xb.at[x, z], b1_s.at[1, 0], b1_r.at[1, 0], (g, left))
    for k in range(1, XS):
        send(xa.at[z, x], xa.at[z, x], a1_s.at[k], a1_r.at[x], (g, inner_at(x + k, z)))
    spread_b(z)
    for k in range(1, XS):
        arrived(xa.at[z, xat(k)], a1_s.at[k], a1_r.at[xat(k)])

    def ring_a(step):
        for p in range(2):
            if step < 3 or p == 0:
                blk = xa.at[zat(-step), pl.ds(2 * p, 2)]
                send(blk, blk, a2_s.at[0, step, p], a2_r.at[0, step, p], (g, right))
            if step < 3 or p == 1:
                blk = xa.at[zat(step), pl.ds(2 * p, 2)]
                send(blk, blk, a2_s.at[1, step, p], a2_r.at[1, step, p], (g, left))

    def came_a(step):
        for p in range(2):
            if step < 4 or p == 0:
                arrived(xa.at[zat(-step), pl.ds(2 * p, 2)], a2_s.at[0, step - 1, p], a2_r.at[0, step - 1, p])
            if step < 4 or p == 1:
                arrived(xa.at[zat(step), pl.ds(2 * p, 2)], a2_s.at[1, step - 1, p], a2_r.at[1, step - 1, p])

    ring_a(0)
    for c in cw:
        c.wait()

    def experts(val):
        tag = val[:, width:].astype(f32)
        out = None
        for e in range(2):
            up = jnp.dot(val[:, :width], wup[e], preferred_element_type=f32)
            hid = up / (1.0 + jnp.exp(-up))
            mask = jnp.where(tag == float(e), 1.0, 0.0)
            hid = (hid * jnp.concatenate([mask] * (hid.shape[1] // TAG), axis=1)).astype(bf16)
            part = jnp.dot(hid, wdn[e], preferred_element_type=f32)
            out = part if out is None else out + part
        return out.astype(bf16)

    def compute_b(xx):
        val = xb[xx].reshape(ZS * half, width + TAG)
        pb[xx] = experts(val).reshape(ZS, half, width)

    def compute_a(z0, z1):
        val = jnp.concatenate(
            [xa[z0].reshape(XS * half, width + TAG), xa[z1].reshape(XS * half, width + TAG)], axis=0
        )
        out = experts(val).reshape(2, XS, half, width)
        pa[z0] = out[0]
        pa[z1] = out[1]

    for step in range(1, 5):
        arrived(xb.at[x, zat(-step)], b1_s.at[0, step - 1], b1_r.at[0, step - 1])
        if step < 4:
            send(xb.at[x, zat(-step)], xb.at[x, zat(-step)], b1_s.at[0, step], b1_r.at[0, step], (g, right))
            arrived(xb.at[x, zat(step)], b1_s.at[1, step - 1], b1_r.at[1, step - 1])
        if step < 3:
            send(xb.at[x, zat(step)], xb.at[x, zat(step)], b1_s.at[1, step], b1_r.at[1, step], (g, left))
        spread_b(zat(-step))
        if step < 4:
            spread_b(zat(step))
    compute_b(x)
    for step in range(1, 5):
        came_a(step)
        if step < 4:
            ring_a(step)
            if step > 1:
                compute_a(zat(step - 1), zat(1 - step))
    compute_a(zat(3), zat(-3))
    compute_a(z, zat(4))

    def add_a(way, step, zz, xs):
        ra_buf[way, step, xs] = (ra_buf[way, step, xs].astype(f32) + pa[zz, xs].astype(f32)).astype(bf16)

    xlo, xhi = pl.ds(0, 2), pl.ds(2, 2)
    send(pa.at[zat(4), xlo], ra_buf.at[0, 0, xlo], ra_s.at[0, 0, 0], ra_r.at[0, 0, 0], (g, right))
    send(pa.at[zat(4), xhi], ra_buf.at[1, 0, xhi], ra_s.at[1, 0, 1], ra_r.at[1, 0, 1], (g, left))
    send(pa.at[zat(3), xhi], ra_buf.at[0, 1, xhi], ra_s.at[0, 1, 1], ra_r.at[0, 1, 1], (g, right))
    send(pa.at[zat(-3), xlo], ra_buf.at[1, 1, xlo], ra_s.at[1, 1, 0], ra_r.at[1, 1, 0], (g, left))

    order = [4, 3, -3, 2, -2, 1, -1, 0]
    for k in range(1, XS):
        xx = xat(k)
        for zd in range(ZS):
            arrived(xb.at[xx, zat(zd)], b2_s.at[k, zat(zd)], b2_r.at[xx, zat(zd)])
        compute_b(xx)
        for zd in order:
            zz = zat(zd)
            send(pb.at[xx, zz], rbx_in.at[x, zz], rbx_s.at[k, zz], rbx_r.at[x, zz], (g, inner_at(x + k, z)))

    def ring_ra(step):
        for way, sgn, dev in ((0, 1, right), (1, -1, left)):
            for p in range(2):
                if step == 1 and p != way:
                    continue
                xs = pl.ds(2 * p, 2)
                arrived(ra_buf.at[way, step - 1, xs], ra_s.at[way, step - 1, p], ra_r.at[way, step - 1, p])
                if step < 4:
                    add_a(way, step - 1, zat(sgn * (4 - step)), xs)
                    send(ra_buf.at[way, step - 1, xs], ra_buf.at[way, step, xs], ra_s.at[way, step, p], ra_r.at[way, step, p], (g, dev))

    def col_sum(zz):
        tot = pb[x, zz].astype(f32)
        for k in range(1, XS):
            arrived(rbx_in.at[xat(k), zz], rbx_s.at[k, zz], rbx_r.at[xat(k), zz])
            tot = tot + rbx_in[xat(k), zz].astype(f32)
        return tot

    for step in range(1, 5):
        ring_ra(step)

    for xx in range(XS):
        rax_out[xx] = (
            pa[z, xx].astype(f32) + ra_buf[0, 3, xx].astype(f32) + ra_buf[1, 3, xx].astype(f32)
        ).astype(bf16)
    for k in range(1, XS):
        send(rax_out.at[xat(k)], rax_in.at[x], rax_s.at[k], rax_r.at[x], (g, inner_at(x + k, z)))

    rb_out[0, 0] = col_sum(zat(4)).astype(bf16)
    send(rb_out.at[0, 0], rb_buf.at[0, 0], rb_s.at[0, 0], rb_r.at[0, 0], (g, right))
    rb_out[1, 0] = col_sum(zat(-3)).astype(bf16)
    send(rb_out.at[1, 0], rb_buf.at[1, 0], rb_s.at[1, 0], rb_r.at[1, 0], (g, left))
    for step in range(1, 4):
        own = col_sum(zat(4 - step))
        arrived(rb_buf.at[0, step - 1], rb_s.at[0, step - 1], rb_r.at[0, step - 1])
        rb_out[0, step] = (own + rb_buf[0, step - 1].astype(f32)).astype(bf16)
        send(rb_out.at[0, step], rb_buf.at[0, step], rb_s.at[0, step], rb_r.at[0, step], (g, right))
        if step < 3:
            own = col_sum(zat(-3 + step))
            arrived(rb_buf.at[1, step - 1], rb_s.at[1, step - 1], rb_r.at[1, step - 1])
            rb_out[1, step] = (own + rb_buf[1, step - 1].astype(f32)).astype(bf16)
            send(rb_out.at[1, step], rb_buf.at[1, step], rb_s.at[1, step], rb_r.at[1, step], (g, left))

    tot = rax_out[x].astype(f32)
    for k in range(1, XS):
        arrived(rax_in.at[xat(k)], rax_s.at[k], rax_r.at[xat(k)])
        tot = tot + rax_in[xat(k)].astype(f32)
    fin = tot.astype(bf16)
    for d in range(groups // 2):
        ret_out[d] = fin[cap * d : cap * (d + 1)]
    tot = col_sum(z)
    for way, step in ((1, 2), (0, 3)):
        arrived(rb_buf.at[way, step], rb_s.at[way, step], rb_r.at[way, step])
        tot = tot + rb_buf[way, step].astype(f32)
    fin = tot.astype(bf16)
    for d in range(groups // 2):
        ret_out[d + groups // 2] = fin[cap * d : cap * (d + 1)]

    @pl.loop(1, groups)
    def _(k):
        d = lax.rem(g + k, groups)
        pltpu.make_async_remote_copy(
            src_ref=ret_out.at[d], dst_ref=ret_in.at[g], send_sem=ret_s.at[d], recv_sem=ret_r.at[g],
            device_id=(d, i), device_id_type=MESH,
        ).start()

    ret_in[g] = ret_out[g]

    @pl.loop(1, groups)
    def _(k):
        d = lax.rem(g + k, groups)
        arrived(ret_in.at[d], ret_s.at[d], ret_r.at[d])

    returned = jnp.concatenate([ret_in[d] for d in range(groups)], axis=0)
    places_t = lax.broadcasted_iota(jnp.int32, (n_rows, slots), 1) == target_col
    combined = jnp.dot(jnp.where(places_t, 1.0, 0.0).astype(bf16), returned, preferred_element_type=f32)
    rw = jnp.sum(jnp.where(eye, rw_ref[...], 0.0), axis=1, keepdims=True)
    o_ref[...] = (combined * rw).astype(o_ref.dtype)

    for c in sent:
        c.wait_send()

    @pl.loop(1, groups)
    def _(k):
        d = lax.rem(g + k, groups)
        for src, dst, s, r in ((out_buf, in_buf, a2a_s, a2a_r), (ret_out, ret_in, ret_s, ret_r)):
            pltpu.make_async_remote_copy(
                src_ref=src.at[d], dst_ref=dst.at[g], send_sem=s.at[d], recv_sem=r.at[g],
                device_id=(d, i), device_id_type=MESH,
            ).wait_send()


def body(pair_rows, group_ids, local_ids, route_weight, w_up, w_down):
    groups = lax.axis_size("group")
    n_rows, width = pair_rows.shape
    cap = 2 * n_rows // groups
    half = groups * cap // 2
    wide = width + TAG
    dma = pltpu.SemaphoreType.DMA
    vmem, hbm = pl.BlockSpec(memory_space=pltpu.VMEM), pl.BlockSpec(memory_space=pl.ANY)
    V = pltpu.VMEM
    scratch = [
        V(w_up.shape, bf16), V(w_down.shape, bf16), dma((2,)),
        V((groups, cap, wide), bf16), V((groups, cap, wide), bf16), dma((groups,)), dma((groups,)),
        V((ZS, XS, half, wide), bf16), V((XS, ZS, half, wide), bf16),
        dma((XS,)), dma((XS,)), dma((2, 4, 2)), dma((2, 4, 2)), dma((2, 4)), dma((2, 4)), dma((XS, ZS)), dma((XS, ZS)),
        V((ZS, XS, half, width), bf16), V((XS, ZS, half, width), bf16),
        dma((2, 4, 2)), dma((2, 4, 2)), V((2, 4, XS, half, width), bf16), dma((XS,)), dma((XS,)),
        V((XS, half, width), bf16), V((XS, half, width), bf16),
        dma((XS, ZS)), dma((XS, ZS)), V((XS, ZS, half, width), bf16),
        dma((2, 4)), dma((2, 4)), V((2, 4, half, width), bf16), V((2, 4, half, width), bf16),
        V((groups, cap, width), bf16), V((groups, cap, width), bf16), dma((groups,)), dma((groups,)),
    ]
    return pl.pallas_call(
        kernel,
        out_shape=jax.ShapeDtypeStruct((n_rows, width), bf16),
        in_specs=[vmem] * 4 + [hbm] * 2,
        out_specs=vmem,
        scratch_shapes=scratch,
        compiler_params=pltpu.CompilerParams(
            collective_id=0, has_side_effects=True, vmem_limit_bytes=56 * 2**20
        ),
        name="routed_experts",
    )(
        pair_rows,
        group_ids.reshape(1, n_rows),
        local_ids.reshape(1, n_rows),
        route_weight.reshape(1, n_rows),
        w_up,
        w_down,
    )


def solution(mesh):
    placed = (
        P(("group", "inner"), None),
        P(("group", "inner"), None),
        P(("group", "inner"), None),
        P(("group", "inner")),
        P("group", None, "inner"),
        P("group", "inner", None),
    )
    return jax.shard_map(
        body, mesh=mesh, in_specs=placed, out_specs=P(("group", "inner"), None), check_vma=False
    )
```

time: 339 us -> 118 us (0.35)
  waiting for transfers between devices: 214 us -> 0 us
  Pallas kernels: 0 us -> 117 us
  blocking collectives: 74.7 us -> 0 us
  local copies, waits for them, and re-layouts: 17.9 us -> 1.47 us
  between operations: 13.5 us -> 0.01 us
  matrix products: 12.1 us -> 0 us
  other arithmetic: 3.41 us -> 0 us
  starting transfers between devices: 3.41 us -> 0 us
    psum x1 -> x0, waiting for transfers between devices: 173 us -> none  [body(): lax.psum(every_term.astype(jnp.bfloat16), 'inner').astype(jnp.float32)]
    pallas_call x0 -> x1, Pallas kernels: none -> 117 us  [body(): pl.pallas_call(kernel, out_shape=jax.ShapeDtypeStruct((n_rows, width), bf...]
    all_to_all x2 -> x0, blocking collectives: 37.5 us -> none  [the longest x1 19 us: body(): lax.all_to_all(send_back, 'group', split_axis=0, concat_axis=0, tiled=True)]
    all_gather x1 -> x0, blocking collectives: 37.2 us -> none  [body(): lax.all_gather(arrived_tags, 'inner', axis=0, tiled=True)]
    all_gather x1 -> x0, waiting for transfers between devices: 34.5 us -> none  [body(): lax.all_gather(arrived, 'inner', axis=0, tiled=True)]
    dot_general x4 -> x0, matrix products: 12.1 us -> none  [the longest x1 9.51 us: body(): jnp.einsum('ref,efd->rd', hidden, w_down, preferred_element_type=jnp.floa...]
    all_gather x2 -> x0, local copies, waits for them, and re-layouts: 8.6 us -> none  [the longest x1 8.52 us: body(): lax.all_gather(arrived, 'inner', axis=0, tiled=True)]
    reshape x5 -> x0, local copies, waits for them, and re-layouts: 8.16 us -> none  [the longest x1 7.19 us: body(): slots = gathered.reshape(inner_size * groups * capacity, model_width)]
  transfers between devices with their start and end apart: 3 -> 0, of which waited for: 3 -> 0; matrix products, arithmetic and copies ran while one was open for 1% -> 0% of each run, Pallas kernels for 0% -> 0%
where the time goes in v1:
time: 118 us
  Pallas kernels  117 us (99%)
  local copies, waits for them, and re-layouts  1.47 us (1%)
    pallas_call x1, Pallas kernels, body(): pl.pallas_call(kernel, out_shape=jax.ShapeDtypeStruct((n_rows, width), bf...  117 us

profile of v1, /device:TPU:1, one launch (start us, length us, event | category | flops | bytes accessed | tf_op | source)
XLA Modules:
  0.0 118.1 jit_solution(10888505359368163572)
XLA Ops:
  0.0 116.6 %routed_experts.1 = bf16[16,2048]{1,0:T(8,128)(2,1)} custom-call(bf16[16,2048]{1,0:T(8,128)(2,1)} %rows_ref.1, s32[1,16]{1,0:T(1,128)} %bitcast.3, s32[1,16]{1,0:T(1,128)} %bitcast.4, f32[1,16]{1,0:T(1,128)} %bitcast.5, bf16[2,2048,256]{2,1,0:T(8,128)(2,1)} %wup_hbm.1, bf16[2,256,2048]{2,1,0:T(8,128)(2,1)} %wdn_hbm.1), custom_call_target="tpu_custom_call" | custom-call | tf_op jit(solution)/shard_map/routed_experts/pallas_call | solution.py:323
  116.6 1.5 %copy.8 = bf16[16,2048]{1,0:T(8,128)(2,1)} copy(bf16[16,2048]{1,0:T(8,128)(2,1)} %routed_experts.1) | data formatting | bytes 131072

commit v2 on v1

--- a/solution.py
+++ b/solution.py
@@ -17,8 +17,8 @@
     rows_ref, gid_ref, lid_ref, rw_ref, wup_hbm, wdn_hbm, o_ref,
     wup, wdn, wsem,
     out_buf, in_buf, a2a_s, a2a_r,
-    xa, xb, a1_s, a1_r, a2_s, a2_r, b1_s, b1_r, b2_s, b2_r,
-    pa, pb, ra_s, ra_r, ra_buf, rax_s, rax_r, rax_out, rax_in,
+    xs, a1_s, a1_r, a2_s, a2_r, b1_s, b1_r, b2_s, b2_r,
+    ps, ra_s, ra_r, ra_buf, rax_s, rax_r, rax_out, rax_in,
     rbx_s, rbx_r, rbx_in, rb_s, rb_r, rb_buf, rb_out,
     ret_out, ret_in, ret_s, ret_r,
 ):
@@ -109,40 +109,44 @@
         arrived(in_buf.at[d], a2a_s.at[d], a2a_r.at[d])
 
     for d in range(groups // 2):
-        xa[z, x, cap * d : cap * (d + 1), :] = in_buf[d]
-        xb[x, z, cap * d : cap * (d + 1), :] = in_buf[d + groups // 2]
+        xs[z, 0, x, cap * d : cap * (d + 1), :] = in_buf[d]
+        xs[z, 1, x, cap * d : cap * (d + 1), :] = in_buf[d + groups // 2]
 
     def spread_b(zz):
         for k in range(1, XS):
-            send(xb.at[x, zz], xb.at[x, zz], b2_s.at[k, zz], b2_r.at[x, zz], (g, inner_at(x + k, z)))
-
-    send(xb.at[x, z], xb.at[x, z], b1_s.at[0, 0], b1_r.at[0, 0], (g, right))
-    send(xb.at[x, z], xb.at[x, z], b1_s.at[1, 0], b1_r.at[1, 0], (g, left))
-    for k in range(1, XS):
-        send(xa.at[z, x], xa.at[z, x], a1_s.at[k], a1_r.at[x], (g, inner_at(x + k, z)))
-    spread_b(z)
-    for k in range(1, XS):
-        arrived(xa.at[z, xat(k)], a1_s.at[k], a1_r.at[xat(k)])
+            send(xs.at[zz, 1, x], xs.at[zz, 1, x], b2_s.at[k, zz], b2_r.at[x, zz], (g, inner_at(x + k, z)))
+
+    def ring_b(step):
+        blk = xs.at[zat(-step), 1, x]
+        send(blk, blk, b1_s.at[0, step], b1_r.at[0, step], (g, right))
+        if step < 3:
+            blk = xs.at[zat(step), 1, x]
+            send(blk, blk, b1_s.at[1, step], b1_r.at[1, step], (g, left))
+
+    def came_b(step):
+        arrived(xs.at[zat(-step), 1, x], b1_s.at[0, step - 1], b1_r.at[0, step - 1])
+        if step < 4:
+            arrived(xs.at[zat(step), 1, x], b1_s.at[1, step - 1], b1_r.at[1, step - 1])
+
+    def came_cols(zz):
+        for k in range(1, XS):
+            arrived(xs.at[zz, 1, xat(k)], b2_s.at[k, zz], b2_r.at[xat(k), zz])
 
     def ring_a(step):
         for p in range(2):
             if step < 3 or p == 0:
-                blk = xa.at[zat(-step), pl.ds(2 * p, 2)]
+                blk = xs.at[zat(-step), 0, pl.ds(2 * p, 2)]
                 send(blk, blk, a2_s.at[0, step, p], a2_r.at[0, step, p], (g, right))
             if step < 3 or p == 1:
-                blk = xa.at[zat(step), pl.ds(2 * p, 2)]
+                blk = xs.at[zat(step), 0, pl.ds(2 * p, 2)]
                 send(blk, blk, a2_s.at[1, step, p], a2_r.at[1, step, p], (g, left))
 
     def came_a(step):
         for p in range(2):
             if step < 4 or p == 0:
-                arrived(xa.at[zat(-step), pl.ds(2 * p, 2)], a2_s.at[0, step - 1, p], a2_r.at[0, step - 1, p])
+                arrived(xs.at[zat(-step), 0, pl.ds(2 * p, 2)], a2_s.at[0, step - 1, p], a2_r.at[0, step - 1, p])
             if step < 4 or p == 1:
-                arrived(xa.at[zat(step), pl.ds(2 * p, 2)], a2_s.at[1, step - 1, p], a2_r.at[1, step - 1, p])
-
-    ring_a(0)
-    for c in cw:
-        c.wait()
+                arrived(xs.at[zat(step), 0, pl.ds(2 * p, 2)], a2_s.at[1, step - 1, p], a2_r.at[1, step - 1, p])
 
     def experts(val):
         tag = val[:, width:].astype(f32)
@@ -156,99 +160,98 @@
             out = part if out is None else out + part
         return out.astype(bf16)
 
-    def compute_b(xx):
-        val = xb[xx].reshape(ZS * half, width + TAG)
-        pb[xx] = experts(val).reshape(ZS, half, width)
-
-    def compute_a(z0, z1):
-        val = jnp.concatenate(
-            [xa[z0].reshape(XS * half, width + TAG), xa[z1].reshape(XS * half, width + TAG)], axis=0
-        )
-        out = experts(val).reshape(2, XS, half, width)
-        pa[z0] = out[0]
-        pa[z1] = out[1]
-
-    for step in range(1, 5):
-        arrived(xb.at[x, zat(-step)], b1_s.at[0, step - 1], b1_r.at[0, step - 1])
-        if step < 4:
-            send(xb.at[x, zat(-step)], xb.at[x, zat(-step)], b1_s.at[0, step], b1_r.at[0, step], (g, right))
-            arrived(xb.at[x, zat(step)], b1_s.at[1, step - 1], b1_r.at[1, step - 1])
-        if step < 3:
-            send(xb.at[x, zat(step)], xb.at[x, zat(step)], b1_s.at[1, step], b1_r.at[1, step], (g, left))
+    def compute(zz):
+        ps[zz] = experts(xs[zz].reshape(2 * XS * half, width + TAG)).reshape(2, XS, half, width)
+
+    def compute_half(zz, h):
+        ps[zz, h] = experts(xs[zz, h].reshape(XS * half, width + TAG)).reshape(XS, half, width)
+
+    def sum_pieces(zz):
+        for k in range(1, XS):
+            send(ps.at[zz, 1, xat(k)], rbx_in.at[x, zz], rbx_s.at[k, zz], rbx_r.at[x, zz], (g, inner_at(x + k, z)))
+
+    ring_b(0)
+    for k in range(1, XS):
+        send(xs.at[z, 0, x], xs.at[z, 0, x], a1_s.at[k], a1_r.at[x], (g, inner_at(x + k, z)))
+    spread_b(z)
+    for k in range(1, XS):
+        arrived(xs.at[z, 0, xat(k)], a1_s.at[k], a1_r.at[xat(k)])
+    ring_a(0)
+    for c in cw:
+        c.wait()
+    for step in range(1, 4):
+        came_b(step)
+        ring_b(step)
         spread_b(zat(-step))
-        if step < 4:
-            spread_b(zat(step))
-    compute_b(x)
-    for step in range(1, 5):
+        spread_b(zat(step))
         came_a(step)
-        if step < 4:
-            ring_a(step)
-            if step > 1:
-                compute_a(zat(step - 1), zat(1 - step))
-    compute_a(zat(3), zat(-3))
-    compute_a(z, zat(4))
-
-    def add_a(way, step, zz, xs):
-        ra_buf[way, step, xs] = (ra_buf[way, step, xs].astype(f32) + pa[zz, xs].astype(f32)).astype(bf16)
-
-    xlo, xhi = pl.ds(0, 2), pl.ds(2, 2)
-    send(pa.at[zat(4), xlo], ra_buf.at[0, 0, xlo], ra_s.at[0, 0, 0], ra_r.at[0, 0, 0], (g, right))
-    send(pa.at[zat(4), xhi], ra_buf.at[1, 0, xhi], ra_s.at[1, 0, 1], ra_r.at[1, 0, 1], (g, left))
-    send(pa.at[zat(3), xhi], ra_buf.at[0, 1, xhi], ra_s.at[0, 1, 1], ra_r.at[0, 1, 1], (g, right))
-    send(pa.at[zat(-3), xlo], ra_buf.at[1, 1, xlo], ra_s.at[1, 1, 0], ra_r.at[1, 1, 0], (g, left))
-
-    order = [4, 3, -3, 2, -2, 1, -1, 0]
-    for k in range(1, XS):
-        xx = xat(k)
-        for zd in range(ZS):
-            arrived(xb.at[xx, zat(zd)], b2_s.at[k, zat(zd)], b2_r.at[xx, zat(zd)])
-        compute_b(xx)
-        for zd in order:
-            zz = zat(zd)
-            send(pb.at[xx, zz], rbx_in.at[x, zz], rbx_s.at[k, zz], rbx_r.at[x, zz], (g, inner_at(x + k, z)))
+        ring_a(step)
+        for zd in sorted({step - 1, 1 - step}):
+            came_cols(zat(zd))
+            compute(zat(zd))
+    came_b(4)
+    spread_b(zat(4))
+    for zd in (3, -3):
+        came_cols(zat(zd))
+        compute(zat(zd))
+    for zd in (0, 1, -1):
+        sum_pieces(zat(zd))
+    came_a(4)
+    compute_half(zat(4), 0)
+
+    def add_a(way, step, zz, sl):
+        ra_buf[way, step, sl] = (ra_buf[way, step, sl].astype(f32) + ps[zz, 0, sl].astype(f32)).astype(bf16)
+
+    lo, hi = pl.ds(0, 2), pl.ds(2, 2)
+    send(ps.at[zat(4), 0, lo], ra_buf.at[0, 0, lo], ra_s.at[0, 0, 0], ra_r.at[0, 0, 0], (g, right))
+    send(ps.at[zat(4), 0, hi], ra_buf.at[1, 0, hi], ra_s.at[1, 0, 1], ra_r.at[1, 0, 1], (g, left))
+    send(ps.at[zat(3), 0, hi], ra_buf.at[0, 1, hi], ra_s.at[0, 1, 1], ra_r.at[0, 1, 1], (g, right))
+    send(ps.at[zat(-3), 0, lo], ra_buf.at[1, 1, lo], ra_s.at[1, 1, 0], ra_r.at[1, 1, 0], (g, left))
+
+    came_cols(zat(4))
+    compute_half(zat(4), 1)
+    for zd in (4, 3, -3, 2, -2):
+        sum_pieces(zat(zd))
 
     def ring_ra(step):
-        for way, sgn, dev in ((0, 1, right), (1, -1, left)):
-            for p in range(2):
+        for p in range(2):
+            for way, sgn, dev in ((0, 1, right), (1, -1, left)):
                 if step == 1 and p != way:
                     continue
-                xs = pl.ds(2 * p, 2)
-                arrived(ra_buf.at[way, step - 1, xs], ra_s.at[way, step - 1, p], ra_r.at[way, step - 1, p])
+                sl = pl.ds(2 * p, 2)
+                arrived(ra_buf.at[way, step - 1, sl], ra_s.at[way, step - 1, p], ra_r.at[way, step - 1, p])
                 if step < 4:
-                    add_a(way, step - 1, zat(sgn * (4 - step)), xs)
-                    send(ra_buf.at[way, step - 1, xs], ra_buf.at[way, step, xs], ra_s.at[way, step, p], ra_r.at[way, step, p], (g, dev))
+                    add_a(way, step - 1, zat(sgn * (4 - step)), sl)
+                    send(ra_buf.at[way, step - 1, sl], ra_buf.at[way, step, sl], ra_s.at[way, step, p], ra_r.at[way, step, p], (g, dev))
 
     def col_sum(zz):
-        tot = pb[x, zz].astype(f32)
+        tot = ps[zz, 1, x].astype(f32)
         for k in range(1, XS):
             arrived(rbx_in.at[xat(k), zz], rbx_s.at[k, zz], rbx_r.at[xat(k), zz])
             tot = tot + rbx_in[xat(k), zz].astype(f32)
         return tot
 
-    for step in range(1, 5):
+    def ring_rb(way, step, zz, dev):
+        tot = col_sum(zz)
+        if step > 0:
+            arrived(rb_buf.at[way, step - 1], rb_s.at[way, step - 1], rb_r.at[way, step - 1])
+            tot = tot + rb_buf[way, step - 1].astype(f32)
+        rb_out[way, step] = tot.astype(bf16)
+        send(rb_out.at[way, step], rb_buf.at[way, step], rb_s.at[way, step], rb_r.at[way, step], (g, dev))
+
+    for step in range(1, 4):
         ring_ra(step)
+        ring_rb(0, step - 1, zat(5 - step), right)
+        ring_rb(1, step - 1, zat(step - 4), left)
+    ring_ra(4)
 
     for xx in range(XS):
         rax_out[xx] = (
-            pa[z, xx].astype(f32) + ra_buf[0, 3, xx].astype(f32) + ra_buf[1, 3, xx].astype(f32)
+            ps[z, 0, xx].astype(f32) + ra_buf[0, 3, xx].astype(f32) + ra_buf[1, 3, xx].astype(f32)
         ).astype(bf16)
     for k in range(1, XS):
         send(rax_out.at[xat(k)], rax_in.at[x], rax_s.at[k], rax_r.at[x], (g, inner_at(x + k, z)))
-
-    rb_out[0, 0] = col_sum(zat(4)).astype(bf16)
-    send(rb_out.at[0, 0], rb_buf.at[0, 0], rb_s.at[0, 0], rb_r.at[0, 0], (g, right))
-    rb_out[1, 0] = col_sum(zat(-3)).astype(bf16)
-    send(rb_out.at[1, 0], rb_buf.at[1, 0], rb_s.at[1, 0], rb_r.at[1, 0], (g, left))
-    for step in range(1, 4):
-        own = col_sum(zat(4 - step))
-        arrived(rb_buf.at[0, step - 1], rb_s.at[0, step - 1], rb_r.at[0, step - 1])
-        rb_out[0, step] = (own + rb_buf[0, step - 1].astype(f32)).astype(bf16)
-        send(rb_out.at[0, step], rb_buf.at[0, step], rb_s.at[0, step], rb_r.at[0, step], (g, right))
-        if step < 3:
-            own = col_sum(zat(-3 + step))
-            arrived(rb_buf.at[1, step - 1], rb_s.at[1, step - 1], rb_r.at[1, step - 1])
-            rb_out[1, step] = (own + rb_buf[1, step - 1].astype(f32)).astype(bf16)
-            send(rb_out.at[1, step], rb_buf.at[1, step], rb_s.at[1, step], rb_r.at[1, step], (g, left))
+    ring_rb(0, 3, zat(1), right)
 
     tot = rax_out[x].astype(f32)
     for k in range(1, XS):
@@ -311,9 +314,9 @@
     scratch = [
         V(w_up.shape, bf16), V(w_down.shape, bf16), dma((2,)),
         V((groups, cap, wide), bf16), V((groups, cap, wide), bf16), dma((groups,)), dma((groups,)),
-        V((ZS, XS, half, wide), bf16), V((XS, ZS, half, wide), bf16),
+        V((ZS, 2, XS, half, wide), bf16),
         dma((XS,)), dma((XS,)), dma((2, 4, 2)), dma((2, 4, 2)), dma((2, 4)), dma((2, 4)), dma((XS, ZS)), dma((XS, ZS)),
-        V((ZS, XS, half, width), bf16), V((XS, ZS, half, width), bf16),
+        V((ZS, 2, XS, half, width), bf16),
         dma((2, 4, 2)), dma((2, 4, 2)), V((2, 4, XS, half, width), bf16), dma((XS,)), dma((XS,)),
         V((XS, half, width), bf16), V((XS, half, width), bf16),
         dma((XS, ZS)), dma((XS, ZS)), V((XS, ZS, half, width), bf16),

time: 118 us -> 106 us (0.90)
  Pallas kernels: 117 us -> 104 us
    pallas_call x1, Pallas kernels: 117 us -> 104 us  [body(): pl.pallas_call(kernel, out_shape=jax.ShapeDtypeStruct((n_rows, width), bf...]
where the time goes in v2:
time: 106 us
  Pallas kernels  104 us (98%)
  local copies, waits for them, and re-layouts  1.47 us (1%)
    pallas_call x1, Pallas kernels, body(): pl.pallas_call(kernel, out_shape=jax.ShapeDtypeStruct((n_rows, width), bf...  104 us

profile of v2, /device:TPU:1, one launch (start us, length us, event | category | flops | bytes accessed | tf_op | source)
XLA Modules:
  0.0 105.8 jit_solution(17221638066674391944)
XLA Ops:
  0.0 104.3 %routed_experts.1 = bf16[16,2048]{1,0:T(8,128)(2,1)} custom-call(bf16[16,2048]{1,0:T(8,128)(2,1)} %rows_ref.1, s32[1,16]{1,0:T(1,128)} %bitcast.3, s32[1,16]{1,0:T(1,128)} %bitcast.4, f32[1,16]{1,0:T(1,128)} %bitcast.5, bf16[2,2048,256]{2,1,0:T(8,128)(2,1)} %wup_hbm.1, bf16[2,256,2048]{2,1,0:T(8,128)(2,1)} %wdn_hbm.1), custom_call_target="tpu_custom_call" | custom-call | tf_op jit(solution)/shard_map/routed_experts/pallas_call | solution.py:326
  104.3 1.5 %copy.8 = bf16[16,2048]{1,0:T(8,128)(2,1)} copy(bf16[16,2048]{1,0:T(8,128)(2,1)} %routed_experts.1) | data formatting | bytes 131072

commit v3 on v2

v3 whole, which is shorter than its diff:
```python
import functools

import jax
import jax.numpy as jnp
from jax import lax
from jax.experimental import pallas as pl
from jax.experimental.pallas import tpu as pltpu
from jax.sharding import PartitionSpec as P

MESH = pl.DeviceIdType.MESH
XS, ZS = 4, 8
TAG = 128
f32, bf16 = jnp.float32, jnp.bfloat16


def kernel(
    rows_ref, gid_ref, lid_ref, rw_ref, wup_hbm, wdn_hbm, o_ref,
    wup, wdn, wsem,
    out_buf, in_buf, a2a_s, a2a_r,
    xa, xb, a1_s, a1_r, a2_s, a2_r, b1_s, b1_r, b2_s, b2_r,
    pa, pb, ra_s, ra_r, ra_buf, rax_s, rax_r, rax_out, rax_in,
    cx_s, cx_r, cx_in, cx_out, rb_s, rb_r, rb_buf, rb_out,
    ret_out, ret_in, ret_s, ret_r,
):
    n_rows, width = rows_ref.shape
    groups, cap = out_buf.shape[0], out_buf.shape[1]
    slots = groups * cap
    half = slots // 2
    wa = xa.shape[-1]
    g = lax.axis_index("group")
    i = lax.axis_index("inner")
    x, z = i // ZS, i % ZS

    def inner_at(xx, zz):
        return lax.rem(xx + XS, XS) * ZS + lax.rem(zz + ZS, ZS)

    right, left = inner_at(x, z + 1), inner_at(x, z - 1)

    def zat(d):
        return lax.rem(z + d + ZS, ZS)

    def xat(k):
        return lax.rem(x + k, XS)

    sent = []

    def send(src, dst, s, r, dev):
        c = pltpu.make_async_remote_copy(
            src_ref=src, dst_ref=dst, send_sem=s, recv_sem=r, device_id=dev, device_id_type=MESH
        )
        c.start()
        sent.append(c)

    def arrived(dst, s, r):
        pltpu.make_async_remote_copy(
            src_ref=dst, dst_ref=dst, send_sem=s, recv_sem=r, device_id=(g, right), device_id_type=MESH
        ).wait_recv()

    cw = [
        pltpu.make_async_copy(wup_hbm, wup, wsem.at[0]),
        pltpu.make_async_copy(wdn_hbm, wdn, wsem.at[1]),
    ]
    for c in cw:
        c.start()

    barrier = pltpu.get_barrier_semaphore()

    @pl.loop(1, groups)
    def _(k):
        pl.semaphore_signal(barrier, inc=1, device_id=(lax.rem(g + k, groups), i), device_id_type=MESH)

    for k in range(1, XS):
        pl.semaphore_signal(barrier, inc=1, device_id=(g, inner_at(x + k, z)), device_id_type=MESH)
    for dev in (right, left):
        pl.semaphore_signal(barrier, inc=1, device_id=(g, dev), device_id_type=MESH)

    gid = gid_ref[...]
    sub = lax.broadcasted_iota(jnp.int32, (n_rows, n_rows), 0)
    lane = lax.broadcasted_iota(jnp.int32, (n_rows, n_rows), 1)
    eye = sub == lane
    gcol = jnp.sum(jnp.where(eye, gid, 0), axis=1, keepdims=True)
    before_row = jnp.where((gcol == gid) & (sub < lane), 1, 0)
    target = gid * cap + jnp.sum(before_row, axis=0, keepdims=True)
    target_col = jnp.sum(jnp.where(eye, target, 0), axis=1, keepdims=True)
    places = lax.broadcasted_iota(jnp.int32, (slots, n_rows), 0) == target
    out_rows = jnp.dot(
        jnp.where(places, 1.0, 0.0).astype(bf16), rows_ref[...], preferred_element_type=f32
    ).astype(bf16)
    tags = jnp.sum(jnp.where(places, lid_ref[...], 0), axis=1, keepdims=True).astype(f32)
    out_tags = jnp.broadcast_to(tags, (slots, TAG)).astype(bf16)
    for d in range(groups):
        out_buf[d, :, :width] = out_rows[cap * d : cap * (d + 1)]
        out_buf[d, :, width:] = out_tags[cap * d : cap * (d + 1)]

    pl.semaphore_wait(barrier, groups - 1 + XS - 1 + 2)

    def far_first(j):
        return lax.rem(g + groups // 2 + (2 * lax.rem(j, 2) - 1) * (j // 2), groups)

    @pl.loop(1, groups)
    def _(j):
        d = far_first(j)
        pltpu.make_async_remote_copy(
            src_ref=out_buf.at[d], dst_ref=in_buf.at[g], send_sem=a2a_s.at[d], recv_sem=a2a_r.at[g],
            device_id=(d, i), device_id_type=MESH,
        ).start()

    in_buf[g] = out_buf[g]

    @pl.loop(1, groups)
    def _(k):
        d = lax.rem(g + k, groups)
        arrived(in_buf.at[d], a2a_s.at[d], a2a_r.at[d])

    for d in range(groups):
        xa[z, x, cap * d : cap * (d + 1), :] = in_buf[d, :, :wa]
        xb[z, x, cap * d : cap * (d + 1), :] = in_buf[d, :, wa:]

    near = (1, 3, 2)
    last = ((0, 1), (3, 2))
    xr, xl = inner_at(x + 1, z), inner_at(x - 1, z)
    rows_of = (pl.ds(0, half), pl.ds(half, half))
    ways = ((0, -1, right), (1, 1, left))

    def passed_on(zd):
        return (3, 1, xr) if zd in (0, -1, -2, -3) else (1, 3, xl)

    def spread_b(zd):
        blk = xb.at[zat(zd), x]
        send(blk, blk, b2_s.at[1, zat(zd)], b2_r.at[x, zat(zd)], (g, xr))
        send(blk, blk, b2_s.at[3, zat(zd)], b2_r.at[x, zat(zd)], (g, xl))

    def came_col(zd, k):
        arrived(xb.at[zat(zd), xat(k)], b2_s.at[2, zat(zd)], b2_r.at[xat(k), zat(zd)])

    def relay_b(zd):
        k, _, dev = passed_on(zd)
        came_col(zd, k)
        blk = xb.at[zat(zd), xat(k)]
        send(blk, blk, b2_s.at[2, zat(zd)], b2_r.at[xat(k), zat(zd)], (g, dev))

    def came_cols(zd):
        came_col(zd, passed_on(zd)[1])
        came_col(zd, 2)

    def ring_b(step):
        for way, sgn, dev in ways:
            blk = xb.at[zat(sgn * step), x]
            if step == 3:
                blk = blk.at[rows_of[way]]
            send(blk, blk, b1_s.at[way, step], b1_r.at[way, step], (g, dev))

    def came_b(step):
        for way, sgn, _ in ways:
            blk = xb.at[zat(sgn * step), x]
            if step == 4:
                blk = blk.at[rows_of[way]]
            arrived(blk, b1_s.at[way, step - 1], b1_r.at[way, step - 1])

    def ring_a(step, k):
        for way, sgn, dev in ways:
            if step < 3 or k in last[way]:
                blk = xa.at[zat(sgn * step), xat(k)]
                send(blk, blk, a2_s.at[way, step, k], a2_r.at[way, step, k], (g, dev))

    def came_a(step, k):
        for way, sgn, _ in ways:
            if step < 4 or k in last[way]:
                arrived(xa.at[zat(sgn * step), xat(k)], a2_s.at[way, step - 1, k], a2_r.at[way, step - 1, k])

    def compute(zd):
        zz = zat(zd)
        va = xa[zz].reshape(XS * slots, wa)
        vb = xb[zz].reshape(XS * slots, width - wa + TAG)
        tag = vb[:, width - wa :].astype(f32)
        out = None
        for e in range(2):
            up = jnp.dot(va, wup[e, :wa], preferred_element_type=f32)
            up = up + jnp.dot(vb[:, : width - wa], wup[e, wa:], preferred_element_type=f32)
            hid = up / (1.0 + jnp.exp(-up))
            mask = jnp.where(tag == float(e), 1.0, 0.0)
            hid = (hid * jnp.concatenate([mask] * (hid.shape[1] // TAG), axis=1)).astype(bf16)
            part = jnp.dot(hid, wdn[e], preferred_element_type=f32)
            out = part if out is None else out + part
        out = out.astype(bf16)
        pa[zz] = out[:, :wa].reshape(XS, slots, wa)
        pb[zz] = out[:, wa:].reshape(XS, slots, width - wa)

    def sums_x(zd):
        zz = zat(zd)
        k, o, dev = passed_on(zd)
        send(pb.at[zz, xat(2)], cx_in.at[0, zz], cx_s.at[0, zz], cx_r.at[0, zz], (g, dev))
        send(pb.at[zz, xat(k)], cx_in.at[1, zz], cx_s.at[1, zz], cx_r.at[1, zz], (g, xr if k == 1 else xl))

    def sums_x_on(zd):
        zz = zat(zd)
        k, o, dev = passed_on(zd)
        arrived(cx_in.at[0, zz], cx_s.at[0, zz], cx_r.at[0, zz])
        cx_out[zz] = (cx_in[0, zz].astype(f32) + pb[zz, xat(o)].astype(f32)).astype(bf16)
        send(cx_out.at[zz], cx_in.at[2, zz], cx_s.at[2, zz], cx_r.at[2, zz], (g, dev))

    def forward_a(step, k):
        came_a(step, k)
        ring_a(step, k)

    def own_a(k):
        arrived(xa.at[z, xat(k)], a1_s.at[k], a1_r.at[xat(k)])
        ring_a(0, k)

    ring_b(0)
    for k in near:
        send(xa.at[z, x], xa.at[z, x], a1_s.at[k], a1_r.at[x], (g, inner_at(x + k, z)))
    ring_a(0, 0)
    spread_b(0)
    own_a(1)
    came_b(1)
    ring_b(1)
    spread_b(-1)
    spread_b(1)
    own_a(3)
    forward_a(1, 0)
    came_b(2)
    ring_b(2)
    spread_b(-2)
    spread_b(2)
    relay_b(0)
    own_a(2)
    forward_a(1, 1)
    came_b(3)
    ring_b(3)
    spread_b(-3)
    spread_b(3)
    forward_a(1, 3)
    forward_a(2, 0)
    relay_b(-1)
    relay_b(1)
    came_b(4)
    spread_b(4)
    for c in cw:
        c.wait()
    forward_a(1, 2)
    forward_a(2, 1)
    came_cols(0)
    compute(0)
    forward_a(2, 3)
    relay_b(-2)
    relay_b(2)
    forward_a(3, 0)
    forward_a(2, 2)
    for zd in (1, -1):
        came_cols(zd)
        compute(zd)
    sums_x(0)
    forward_a(3, 1)
    relay_b(-3)
    relay_b(3)
    forward_a(3, 3)
    forward_a(3, 2)
    for zd in (2, -2):
        came_cols(zd)
        compute(zd)
    relay_b(4)
    sums_x(1)
    sums_x(-1)
    for zd in (3, -3):
        came_cols(zd)
        compute(zd)
    sums_x_on(0)
    for k in (0, *near):
        came_a(4, k)
    came_cols(4)
    compute(4)

    order = (2, 1, 3, 0)
    first = (order[:2], order[2:])

    def start_ra(step, way, zd, dev, ks):
        for k in ks:
            send(pa.at[zat(zd), xat(k)], ra_buf.at[way, step, k], ra_s.at[way, step, k], ra_r.at[way, step, k], (g, dev))

    start_ra(0, 0, 4, right, first[0])
    start_ra(0, 1, 4, left, first[1])
    sums_x(4)
    start_ra(1, 0, 3, right, first[1])
    start_ra(1, 1, -3, left, first[0])
    for zd in (3, -3, 2, -2):
        sums_x(zd)
    sums_x_on(1)
    sums_x_on(-1)

    def came_ra(way, step, k):
        arrived(ra_buf.at[way, step - 1, k], ra_s.at[way, step - 1, k], ra_r.at[way, step - 1, k])
        return ra_buf[way, step - 1, k].astype(f32)

    def ring_ra(step, places=range(XS)):
        for j in places:
            for way, sgn, dev in ((0, 1, right), (1, -1, left)):
                k = (*first[1 - way], *first[way])[j]
                if step == 1 and k not in first[way]:
                    continue
                zz = zat(sgn * (4 - step))
                ra_buf[way, step - 1, k] = (came_ra(way, step, k) + pa[zz, xat(k)].astype(f32)).astype(bf16)
                send(ra_buf.at[way, step - 1, k], ra_buf.at[way, step, k], ra_s.at[way, step, k], ra_r.at[way, step, k], (g, dev))

    def col_sum(zz):
        for j in (1, 2):
            arrived(cx_in.at[j, zz], cx_s.at[j, zz], cx_r.at[j, zz])
        return pb[zz, x].astype(f32) + cx_in[1, zz].astype(f32) + cx_in[2, zz].astype(f32)

    def came_rb(way, step):
        dst = rb_buf.at[way, step]
        if step == 0:
            dst = dst.at[rows_of[way]]
        arrived(dst, rb_s.at[way, step], rb_r.at[way, step])

    def send_rb(way, step):
        src, dst = rb_out.at[way, step], rb_buf.at[way, step]
        if step == 0:
            src, dst = src.at[rows_of[way]], dst.at[rows_of[way]]
        send(src, dst, rb_s.at[way, step], rb_r.at[way, step], (g, (right, left)[way]))

    def start_rb():
        tot = col_sum(zat(4)).astype(bf16)
        for way in range(2):
            rb_out[way, 0] = tot
            send_rb(way, 0)

    def ring_rb(step):
        for way, sgn in ((0, 1), (1, -1)):
            tot = col_sum(zat(sgn * (4 - step)))
            came_rb(way, step - 1)
            if step == 1:
                rb_out[way, 1] = tot.astype(bf16)
                mine = slice(half * way, half * (way + 1))
                rb_out[way, 1, mine] = (tot[mine] + rb_buf[way, 0, mine].astype(f32)).astype(bf16)
            else:
                rb_out[way, step] = (tot + rb_buf[way, step - 1].astype(f32)).astype(bf16)
            send_rb(way, step)

    ring_ra(1)
    sums_x_on(4)
    ring_ra(2, (0, 1))
    sums_x_on(3)
    sums_x_on(-3)
    start_rb()
    ring_ra(2, (2, 3))
    sums_x_on(2)
    sums_x_on(-2)
    ring_rb(1)
    ring_ra(3, (0, 1))
    ring_rb(2)
    ring_ra(3, (2, 3))
    ring_rb(3)
    for k in order:
        rax_out[k] = (pa[z, xat(k)].astype(f32) + came_ra(0, 4, k) + came_ra(1, 4, k)).astype(bf16)
        if k:
            send(rax_out.at[k], rax_in.at[x], rax_s.at[k], rax_r.at[x], (g, inner_at(x + k, z)))

    def back(part, fin):
        for d in range(groups):
            ret_out[part][d] = fin[cap * d : cap * (d + 1)]

        @pl.loop(1, groups)
        def _(j):
            d = far_first(j)
            pltpu.make_async_remote_copy(
                src_ref=ret_out[part].at[d], dst_ref=ret_in[part].at[g], send_sem=ret_s.at[part, d],
                recv_sem=ret_r.at[part, g], device_id=(d, i), device_id_type=MESH,
            ).start()

        ret_in[part][g] = ret_out[part][g]

    tot = col_sum(z)
    for way in range(2):
        came_rb(way, 3)
        tot = tot + rb_buf[way, 3].astype(f32)
    back(1, tot.astype(bf16))
    tot = rax_out[0].astype(f32)
    for k in near:
        arrived(rax_in.at[xat(k)], rax_s.at[k], rax_r.at[xat(k)])
        tot = tot + rax_in[xat(k)].astype(f32)
    back(0, tot.astype(bf16))

    places_t = jnp.where(
        lax.broadcasted_iota(jnp.int32, (n_rows, slots), 1) == target_col, 1.0, 0.0
    ).astype(bf16)
    rw = jnp.sum(jnp.where(eye, rw_ref[...], 0.0), axis=1, keepdims=True)
    for part, columns in ((1, slice(wa, width)), (0, slice(0, wa))):

        @pl.loop(1, groups)
        def _(k):
            d = lax.rem(g + k, groups)
            arrived(ret_in[part].at[d], ret_s.at[part, d], ret_r.at[part, d])

        returned = jnp.concatenate([ret_in[part][d] for d in range(groups)], axis=0)
        combined = jnp.dot(places_t, returned, preferred_element_type=f32)
        o_ref[:, columns] = (combined * rw).astype(o_ref.dtype)

    for c in sent:
        c.wait_send()

    @pl.loop(1, groups)
    def _(k):
        d = lax.rem(g + k, groups)
        moved = [(out_buf, in_buf, a2a_s.at[d], a2a_r.at[g])]
        moved += [(ret_out[p], ret_in[p], ret_s.at[p, d], ret_r.at[p, g]) for p in range(2)]
        for src, dst, s, r in moved:
            pltpu.make_async_remote_copy(
                src_ref=src.at[d], dst_ref=dst.at[g], send_sem=s, recv_sem=r,
                device_id=(d, i), device_id_type=MESH,
            ).wait_send()


def body(pair_rows, group_ids, local_ids, route_weight, w_up, w_down):
    groups = lax.axis_size("group")
    n_rows, width = pair_rows.shape
    cap = 2 * n_rows // groups
    slots = groups * cap
    wa = 7 * width // 16
    wb = width - wa
    wide = width + TAG
    dma = pltpu.SemaphoreType.DMA
    vmem, hbm = pl.BlockSpec(memory_space=pltpu.VMEM), pl.BlockSpec(memory_space=pl.ANY)
    V = pltpu.VMEM
    scratch = [
        V(w_up.shape, bf16), V(w_down.shape, bf16), dma((2,)),
        V((groups, cap, wide), bf16), V((groups, cap, wide), bf16), dma((groups,)), dma((groups,)),
        V((ZS, XS, slots, wa), bf16), V((ZS, XS, slots, wb + TAG), bf16),
        dma((XS,)), dma((XS,)), dma((2, 4, XS)), dma((2, 4, XS)), dma((2, 4)), dma((2, 4)), dma((XS, ZS)), dma((XS, ZS)),
        V((ZS, XS, slots, wa), bf16), V((ZS, XS, slots, wb), bf16),
        dma((2, 4, XS)), dma((2, 4, XS)), V((2, 4, XS, slots, wa), bf16), dma((XS,)), dma((XS,)),
        V((XS, slots, wa), bf16), V((XS, slots, wa), bf16),
        dma((3, ZS)), dma((3, ZS)), V((3, ZS, slots, wb), bf16), V((ZS, slots, wb), bf16),
        dma((2, 4)), dma((2, 4)), V((2, 4, slots, wb), bf16), V((2, 4, slots, wb), bf16),
        [V((groups, cap, w), bf16) for w in (wa, wb)], [V((groups, cap, w), bf16) for w in (wa, wb)],
        dma((2, groups)), dma((2, groups)),
    ]
    return pl.pallas_call(
        kernel,
        out_shape=jax.ShapeDtypeStruct((n_rows, width), bf16),
        in_specs=[vmem] * 4 + [hbm] * 2,
        out_specs=vmem,
        scratch_shapes=scratch,
        compiler_params=pltpu.CompilerParams(
            collective_id=0, has_side_effects=True, vmem_limit_bytes=56 * 2**20
        ),
        name="routed_experts",
    )(
        pair_rows,
        group_ids.reshape(1, n_rows),
        local_ids.reshape(1, n_rows),
        route_weight.reshape(1, n_rows),
        w_up,
        w_down,
    )


def solution(mesh):
    placed = (
        P(("group", "inner"), None),
        P(("group", "inner"), None),
        P(("group", "inner"), None),
        P(("group", "inner")),
        P("group", None, "inner"),
        P("group", "inner", None),
    )
    return jax.shard_map(
        body, mesh=mesh, in_specs=placed, out_specs=P(("group", "inner"), None), check_vma=False
    )
```

time: 106 us -> 96.2 us (0.908)
  Pallas kernels: 104 us -> 94.5 us
    pallas_call x1, Pallas kernels: 104 us -> 94.5 us  [body(): pl.pallas_call(kernel, out_shape=jax.ShapeDtypeStruct((n_rows, width), bf...]
where the time goes in v3:
time: 96.2 us; the launch traced here: 96 us
  Pallas kernels  94.5 us (98%)
  local copies, waits for them, and re-layouts  1.47 us (2%)
    pallas_call x1, Pallas kernels, body(): pl.pallas_call(kernel, out_shape=jax.ShapeDtypeStruct((n_rows, width), bf...  94.5 us

profile of v3, /device:TPU:1, one launch (start us, length us, event | category | flops | bytes accessed | tf_op | source)
XLA Modules:
  0.0 96.0 jit_solution(4234510226800211753)
XLA Ops:
  0.0 94.5 %routed_experts.1 = bf16[16,2048]{1,0:T(8,128)(2,1)} custom-call(bf16[16,2048]{1,0:T(8,128)(2,1)} %rows_ref.1, s32[1,16]{1,0:T(1,128)} %bitcast.3, s32[1,16]{1,0:T(1,128)} %bitcast.4, f32[1,16]{1,0:T(1,128)} %bitcast.5, bf16[2,2048,256]{2,1,0:T(8,128)(2,1)} %wup_hbm.1, bf16[2,256,2048]{2,1,0:T(8,128)(2,1)} %wdn_hbm.1), custom_call_target="tpu_custom_call" | custom-call | tf_op jit(solution)/shard_map/routed_experts/pallas_call | solution.py:438
  94.6 1.5 %copy.8 = bf16[16,2048]{1,0:T(8,128)(2,1)} copy(bf16[16,2048]{1,0:T(8,128)(2,1)} %routed_experts.1) | data formatting | bytes 131072

commit v4 on v3

--- a/solution.py
+++ b/solution.py
@@ -10,12 +10,13 @@
 MESH = pl.DeviceIdType.MESH
 XS, ZS = 4, 8
 TAG = 128
+DIRECT = (4,)
 f32, bf16 = jnp.float32, jnp.bfloat16
 
 
 def kernel(
-    rows_ref, gid_ref, lid_ref, rw_ref, wup_hbm, wdn_hbm, o_ref,
-    wup, wdn, wsem,
+    rows_hbm, gid_hbm, lid_hbm, rw_hbm, wup_hbm, wdn_hbm, o_ref,
+    rows_ref, gid_ref, lid_ref, rw_ref, isem, wup, wdn, wsem,
     out_buf, in_buf, a2a_s, a2a_r,
     xa, xb, a1_s, a1_r, a2_s, a2_r, b1_s, b1_r, b2_s, b2_r,
     pa, pb, ra_s, ra_r, ra_buf, rax_s, rax_r, rax_out, rax_in,
@@ -56,6 +57,28 @@
             src_ref=dst, dst_ref=dst, send_sem=s, recv_sem=r, device_id=(g, right), device_id_type=MESH
         ).wait_recv()
 
+    barrier = pltpu.get_barrier_semaphore()
+
+    def far_first(j):
+        return lax.rem(g + groups // 2 + (2 * lax.rem(j, 2) - 1) * (j // 2), groups)
+
+    @pl.loop(1, groups)
+    def _(j):
+        pl.semaphore_signal(barrier, inc=1, device_id=(far_first(j), i), device_id_type=MESH)
+
+    for k in range(1, XS):
+        pl.semaphore_signal(barrier, inc=1, device_id=(g, inner_at(x + k, z)), device_id_type=MESH)
+    for dev in (right, left):
+        pl.semaphore_signal(barrier, inc=1, device_id=(g, dev), device_id_type=MESH)
+
+    cin = [
+        pltpu.make_async_copy(src, dst, isem.at[n])
+        for n, (src, dst) in enumerate(
+            ((gid_hbm, gid_ref), (lid_hbm, lid_ref), (rw_hbm, rw_ref), (rows_hbm, rows_ref))
+        )
+    ]
+    for c in cin:
+        c.start()
     cw = [
         pltpu.make_async_copy(wup_hbm, wup, wsem.at[0]),
         pltpu.make_async_copy(wdn_hbm, wdn, wsem.at[1]),
@@ -63,16 +86,8 @@
     for c in cw:
         c.start()
 
-    barrier = pltpu.get_barrier_semaphore()
-
-    @pl.loop(1, groups)
-    def _(k):
-        pl.semaphore_signal(barrier, inc=1, device_id=(lax.rem(g + k, groups), i), device_id_type=MESH)
-
-    for k in range(1, XS):
-        pl.semaphore_signal(barrier, inc=1, device_id=(g, inner_at(x + k, z)), device_id_type=MESH)
-    for dev in (right, left):
-        pl.semaphore_signal(barrier, inc=1, device_id=(g, dev), device_id_type=MESH)
+    for c in cin:
+        c.wait()
 
     gid = gid_ref[...]
     sub = lax.broadcasted_iota(jnp.int32, (n_rows, n_rows), 0)
@@ -94,9 +109,6 @@
 
     pl.semaphore_wait(barrier, groups - 1 + XS - 1 + 2)
 
-    def far_first(j):
-        return lax.rem(g + groups // 2 + (2 * lax.rem(j, 2) - 1) * (j // 2), groups)
-
     @pl.loop(1, groups)
     def _(j):
         d = far_first(j)
@@ -129,17 +141,23 @@
         blk = xb.at[zat(zd), x]
         send(blk, blk, b2_s.at[1, zat(zd)], b2_r.at[x, zat(zd)], (g, xr))
         send(blk, blk, b2_s.at[3, zat(zd)], b2_r.at[x, zat(zd)], (g, xl))
+        if zd in DIRECT:
+            send(blk, blk, b2_s.at[2, zat(zd)], b2_r.at[x, zat(zd)], (g, inner_at(x + 2, z)))
 
     def came_col(zd, k):
         arrived(xb.at[zat(zd), xat(k)], b2_s.at[2, zat(zd)], b2_r.at[xat(k), zat(zd)])
 
     def relay_b(zd):
+        if zd in DIRECT:
+            return
         k, _, dev = passed_on(zd)
         came_col(zd, k)
         blk = xb.at[zat(zd), xat(k)]
         send(blk, blk, b2_s.at[2, zat(zd)], b2_r.at[xat(k), zat(zd)], (g, dev))
 
     def came_cols(zd):
+        if zd in DIRECT:
+            came_col(zd, passed_on(zd)[0])
         came_col(zd, passed_on(zd)[1])
         came_col(zd, 2)
 
@@ -188,11 +206,17 @@
 
     def sums_x(zd):
         zz = zat(zd)
+        if zd in DIRECT:
+            for k in near:
+                send(pb.at[zz, xat(k)], cx_in.at[k - 1, zz], cx_s.at[k - 1, zz], cx_r.at[k - 1, zz], (g, inner_at(x + k, z)))
+            return
         k, o, dev = passed_on(zd)
         send(pb.at[zz, xat(2)], cx_in.at[0, zz], cx_s.at[0, zz], cx_r.at[0, zz], (g, dev))
         send(pb.at[zz, xat(k)], cx_in.at[1, zz], cx_s.at[1, zz], cx_r.at[1, zz], (g, xr if k == 1 else xl))
 
     def sums_x_on(zd):
+        if zd in DIRECT:
+            return
         zz = zat(zd)
         k, o, dev = passed_on(zd)
         arrived(cx_in.at[0, zz], cx_s.at[0, zz], cx_r.at[0, zz])
@@ -259,9 +283,6 @@
     for zd in (2, -2):
         came_cols(zd)
         compute(zd)
-    relay_b(4)
-    sums_x(1)
-    sums_x(-1)
     for zd in (3, -3):
         came_cols(zd)
         compute(zd)
@@ -278,15 +299,12 @@
         for k in ks:
             send(pa.at[zat(zd), xat(k)], ra_buf.at[way, step, k], ra_s.at[way, step, k], ra_r.at[way, step, k], (g, dev))
 
+    sums_x(4)
     start_ra(0, 0, 4, right, first[0])
     start_ra(0, 1, 4, left, first[1])
-    sums_x(4)
+    sums_x(3)
     start_ra(1, 0, 3, right, first[1])
     start_ra(1, 1, -3, left, first[0])
-    for zd in (3, -3, 2, -2):
-        sums_x(zd)
-    sums_x_on(1)
-    sums_x_on(-1)
 
     def came_ra(way, step, k):
         arrived(ra_buf.at[way, step - 1, k], ra_s.at[way, step - 1, k], ra_r.at[way, step - 1, k])
@@ -302,10 +320,13 @@
                 ra_buf[way, step - 1, k] = (came_ra(way, step, k) + pa[zz, xat(k)].astype(f32)).astype(bf16)
                 send(ra_buf.at[way, step - 1, k], ra_buf.at[way, step, k], ra_s.at[way, step, k], ra_r.at[way, step, k], (g, dev))
 
-    def col_sum(zz):
-        for j in (1, 2):
+    def col_sum(zd):
+        zz = zat(zd)
+        tot = pb[zz, x].astype(f32)
+        for j in (0, 1, 2) if zd in DIRECT else (1, 2):
             arrived(cx_in.at[j, zz], cx_s.at[j, zz], cx_r.at[j, zz])
-        return pb[zz, x].astype(f32) + cx_in[1, zz].astype(f32) + cx_in[2, zz].astype(f32)
+            tot = tot + cx_in[j, zz].astype(f32)
+        return tot
 
     def came_rb(way, step):
         dst = rb_buf.at[way, step]
@@ -320,14 +341,14 @@
         send(src, dst, rb_s.at[way, step], rb_r.at[way, step], (g, (right, left)[way]))
 
     def start_rb():
-        tot = col_sum(zat(4)).astype(bf16)
+        tot = col_sum(4).astype(bf16)
         for way in range(2):
             rb_out[way, 0] = tot
             send_rb(way, 0)
 
     def ring_rb(step):
         for way, sgn in ((0, 1), (1, -1)):
-            tot = col_sum(zat(sgn * (4 - step)))
+            tot = col_sum(sgn * (4 - step))
             came_rb(way, step - 1)
             if step == 1:
                 rb_out[way, 1] = tot.astype(bf16)
@@ -337,18 +358,24 @@
                 rb_out[way, step] = (tot + rb_buf[way, step - 1].astype(f32)).astype(bf16)
             send_rb(way, step)
 
+    sums_x(-3)
     ring_ra(1)
-    sums_x_on(4)
+    sums_x_on(3)
+    start_rb()
+    sums_x(2)
     ring_ra(2, (0, 1))
-    sums_x_on(3)
     sums_x_on(-3)
-    start_rb()
+    sums_x(-2)
+    ring_rb(1)
     ring_ra(2, (2, 3))
     sums_x_on(2)
+    sums_x(1)
     sums_x_on(-2)
-    ring_rb(1)
+    sums_x(-1)
+    ring_rb(2)
     ring_ra(3, (0, 1))
-    ring_rb(2)
+    sums_x_on(1)
+    sums_x_on(-1)
     ring_ra(3, (2, 3))
     ring_rb(3)
     for k in order:
@@ -370,7 +397,7 @@
 
         ret_in[part][g] = ret_out[part][g]
 
-    tot = col_sum(z)
+    tot = col_sum(0)
     for way in range(2):
         came_rb(way, 3)
         tot = tot + rb_buf[way, 3].astype(f32)
@@ -380,21 +407,6 @@
         arrived(rax_in.at[xat(k)], rax_s.at[k], rax_r.at[xat(k)])
         tot = tot + rax_in[xat(k)].astype(f32)
     back(0, tot.astype(bf16))
-
-    places_t = jnp.where(
-        lax.broadcasted_iota(jnp.int32, (n_rows, slots), 1) == target_col, 1.0, 0.0
-    ).astype(bf16)
-    rw = jnp.sum(jnp.where(eye, rw_ref[...], 0.0), axis=1, keepdims=True)
-    for part, columns in ((1, slice(wa, width)), (0, slice(0, wa))):
-
-        @pl.loop(1, groups)
-        def _(k):
-            d = lax.rem(g + k, groups)
-            arrived(ret_in[part].at[d], ret_s.at[part, d], ret_r.at[part, d])
-
-        returned = jnp.concatenate([ret_in[part][d] for d in range(groups)], axis=0)
-        combined = jnp.dot(places_t, returned, preferred_element_type=f32)
-        o_ref[:, columns] = (combined * rw).astype(o_ref.dtype)
 
     for c in sent:
         c.wait_send()
@@ -410,19 +422,35 @@
                 device_id=(d, i), device_id_type=MESH,
             ).wait_send()
 
+    places_t = jnp.where(
+        lax.broadcasted_iota(jnp.int32, (n_rows, slots), 1) == target_col, 1.0, 0.0
+    ).astype(bf16)
+    rw = jnp.sum(jnp.where(eye, rw_ref[...], 0.0), axis=1, keepdims=True)
+    for part, columns in ((1, slice(wa, width)), (0, slice(0, wa))):
+
+        @pl.loop(1, groups)
+        def _(k):
+            d = lax.rem(g + k, groups)
+            arrived(ret_in[part].at[d], ret_s.at[part, d], ret_r.at[part, d])
+
+        returned = jnp.concatenate([ret_in[part][d] for d in range(groups)], axis=0)
+        combined = jnp.dot(places_t, returned, preferred_element_type=f32)
+        o_ref[:, columns] = (combined * rw).astype(o_ref.dtype)
+
 
 def body(pair_rows, group_ids, local_ids, route_weight, w_up, w_down):
     groups = lax.axis_size("group")
     n_rows, width = pair_rows.shape
     cap = 2 * n_rows // groups
     slots = groups * cap
-    wa = 7 * width // 16
+    wa = 8 * width // 16
     wb = width - wa
     wide = width + TAG
     dma = pltpu.SemaphoreType.DMA
     vmem, hbm = pl.BlockSpec(memory_space=pltpu.VMEM), pl.BlockSpec(memory_space=pl.ANY)
     V = pltpu.VMEM
     scratch = [
+        V((n_rows, width), bf16), V((1, n_rows), jnp.int32), V((1, n_rows), jnp.int32), V((1, n_rows), f32), dma((4,)),
         V(w_up.shape, bf16), V(w_down.shape, bf16), dma((2,)),
         V((groups, cap, wide), bf16), V((groups, cap, wide), bf16), dma((groups,)), dma((groups,)),
         V((ZS, XS, slots, wa), bf16), V((ZS, XS, slots, wb + TAG), bf16),
@@ -438,7 +466,7 @@
     return pl.pallas_call(
         kernel,
         out_shape=jax.ShapeDtypeStruct((n_rows, width), bf16),
-        in_specs=[vmem] * 4 + [hbm] * 2,
+        in_specs=[hbm] * 6,
         out_specs=vmem,
         scratch_shapes=scratch,
         compiler_params=pltpu.CompilerParams(

time: 96.2 us -> 93.2 us (0.969)
  Pallas kernels: 94.5 us -> 91.6 us
    pallas_call x1, Pallas kernels: 94.5 us -> 91.6 us  [body(): pl.pallas_call(kernel, out_shape=jax.ShapeDtypeStruct((n_rows, width), bf...]
where the time goes in v4:
time: 93.2 us; the launch traced here: 93.1 us
  Pallas kernels  91.6 us (98%)
  local copies, waits for them, and re-layouts  1.47 us (2%)
    pallas_call x1, Pallas kernels, body(): pl.pallas_call(kernel, out_shape=jax.ShapeDtypeStruct((n_rows, width), bf...  91.6 us

profile of v4, /device:TPU:1, one launch (start us, length us, event | category | flops | bytes accessed | tf_op | source)
XLA Modules:
  0.0 93.1 jit_solution(2179426799664887539)
XLA Ops:
  0.0 91.6 %routed_experts.1 = bf16[16,2048]{1,0:T(8,128)(2,1)} custom-call(bf16[16,2048]{1,0:T(8,128)(2,1)} %rows_hbm.1, s32[1,16]{1,0:T(1,128)} %bitcast.3, s32[1,16]{1,0:T(1,128)} %bitcast.4, f32[1,16]{1,0:T(1,128)} %bitcast.5, bf16[2,2048,256]{2,1,0:T(8,128)(2,1)} %wup_hbm.1, bf16[2,256,2048]{2,1,0:T(8,128)(2,1)} %wdn_hbm.1), custom_call_target="tpu_custom_call" | custom-call | tf_op jit(solution)/shard_map/routed_experts/pallas_call | solution.py:466
  91.6 1.5 %copy.8 = bf16[16,2048]{1,0:T(8,128)(2,1)} copy(bf16[16,2048]{1,0:T(8,128)(2,1)} %routed_experts.1) | data formatting | bytes 131072

commit v5 on v4

--- a/solution.py
+++ b/solution.py
@@ -271,18 +271,20 @@
     relay_b(2)
     forward_a(3, 0)
     forward_a(2, 2)
-    for zd in (1, -1):
-        came_cols(zd)
-        compute(zd)
+    came_cols(1)
+    compute(1)
+    forward_a(3, 1)
+    came_cols(-1)
+    compute(-1)
     sums_x(0)
-    forward_a(3, 1)
     relay_b(-3)
     relay_b(3)
     forward_a(3, 3)
+    came_cols(2)
+    compute(2)
     forward_a(3, 2)
-    for zd in (2, -2):
-        came_cols(zd)
-        compute(zd)
+    came_cols(-2)
+    compute(-2)
     for zd in (3, -3):
         came_cols(zd)
         compute(zd)

time: 93.2 us -> 93.2 us (level)
  no operation moved by 1% of the time
where the time goes in v5:
time: 93.2 us; the launch traced here: 93.1 us
  Pallas kernels  91.6 us (98%)
  local copies, waits for them, and re-layouts  1.47 us (2%)
    pallas_call x1, Pallas kernels, body(): pl.pallas_call(kernel, out_shape=jax.ShapeDtypeStruct((n_rows, width), bf...  91.6 us

profile of v5, /device:TPU:1, one launch (start us, length us, event | category | flops | bytes accessed | tf_op | source)
XLA Modules:
  0.0 93.1 jit_solution(3818450651115253632)
XLA Ops:
  0.0 91.6 %routed_experts.1 = bf16[16,2048]{1,0:T(8,128)(2,1)} custom-call(bf16[16,2048]{1,0:T(8,128)(2,1)} %rows_hbm.1, s32[1,16]{1,0:T(1,128)} %bitcast.3, s32[1,16]{1,0:T(1,128)} %bitcast.4, f32[1,16]{1,0:T(1,128)} %bitcast.5, bf16[2,2048,256]{2,1,0:T(8,128)(2,1)} %wup_hbm.1, bf16[2,256,2048]{2,1,0:T(8,128)(2,1)} %wdn_hbm.1), custom_call_target="tpu_custom_call" | custom-call | tf_op jit(solution)/shard_map/routed_experts/pallas_call | solution.py:468
  91.6 1.5 %copy.8 = bf16[16,2048]{1,0:T(8,128)(2,1)} copy(bf16[16,2048]{1,0:T(8,128)(2,1)} %routed_experts.1) | data formatting | bytes 131072
